TPU v7x, 128 devices: a whole 4x4x4 slice. The times are simulated.
128 devices in a mesh: req: 16 (over x, z), mlp: 8 (over y, core).
Axes of the slice: x: 4, y: 4, z: 4, core: 2. Of those that a mesh axis runs over, the one named last changes fastest.
Arguments:
- patches: bfloat16 [15360, 4096], P('req'), may hold values from -6 to 6
- norm_gain: float32 [4096], replicated, may hold values from 0.25 to 1.75
- norm_bias: float32 [4096], replicated, may hold values from -3 to 3
- gate_weight: bfloat16 [4096, 8192], P(None, ('req', 'mlp')), may hold values from -0.09375 to 0.09375
- up_weight: bfloat16 [4096, 8192], P(None, ('req', 'mlp')), may hold values from -0.09375 to 0.09375
- down_weight: bfloat16 [4096, 8192], P(None, ('req', 'mlp')), may hold values from -0.0625 to 0.0625
- layer_scale: float32 [4096], replicated, may hold values from 0.25 to 2.5
- projection: bfloat16 [4, 4096, 4096], P(None, 'mlp', 'req'), may hold values from -0.046875 to 0.046875
- text_rows: bfloat16 [65536, 4096], P(('req', 'mlp')), may hold values from -6 to 6
- destination: int32 [3840], replicated, may hold values from -1 to 65535, as said below
Outputs:
- patch_out: bfloat16 [15360, 4096], P('req', 'mlp')
- streams: bfloat16 [65536, 4096], P(('req', 'mlp'))
Inputs may be any that keep to these rules, and one draw needn't show every extreme that they name: `destination`: values other than -1 are distinct positions; the positions landing in one piece of 512 consecutive positions (a stream holds 8 pieces) form one run of consecutive positions, at least one and at most 30 of them, and some piece receives exactly 30.
All inputs are finite; a program needn't handle non-finite values.
Results may differ from a plain program's by a relative error of at most 0.015.
Values may be sent and summed in bfloat16 or wider, within the bound.
No kernel may reach another device: no remote copies, remote signals or barrier semaphores. Data moves between devices by JAX's collectives and lax.ppermute only.
A program may use at most 128 MiB of HBM per device.

v0:
```python
import jax
import jax.numpy as jnp
from jax import lax
from jax.sharding import PartitionSpec as P


def layer_norm(values, norm_gain, norm_bias):
    row_mean = jnp.mean(values, axis=-1, keepdims=True)
    centred = values - row_mean
    variance = jnp.mean(centred * centred, axis=-1, keepdims=True)
    return centred * lax.rsqrt(variance + 1e-06) * norm_gain + norm_bias


def shards(
    patches,
    norm_gain,
    norm_bias,
    gate_weight,
    up_weight,
    down_weight,
    layer_scale,
    projection,
    text_rows,
    destination,
):
    req_count = lax.axis_size("req")
    mlp_count = lax.axis_size("mlp")
    req_index = lax.axis_index("req")
    mlp_index = lax.axis_index("mlp")
    rows_here, model_width = patches.shape
    feat_width = model_width // mlp_count
    inputs = patches.astype(jnp.float32)
    normed = layer_norm(inputs, norm_gain, norm_bias).astype(jnp.bfloat16)
    gate_act = jnp.dot(
        normed,
        lax.all_gather(gate_weight, "req", axis=1, tiled=True),
        preferred_element_type=jnp.float32,
    )
    up_act = jnp.dot(
        normed,
        lax.all_gather(up_weight, "req", axis=1, tiled=True),
        preferred_element_type=jnp.float32,
    )
    hidden = (jax.nn.silu(gate_act) * up_act).astype(jnp.bfloat16)
    ffn_local = lax.dot_general(
        hidden,
        lax.all_gather(down_weight, "req", axis=1, tiled=True),
        (((1,), (1,)), ((), ())),
        preferred_element_type=jnp.float32,
    )
    partial_value = lax.optimization_barrier(ffn_local.astype(jnp.bfloat16)).astype(jnp.float32)
    ffn_feats = lax.psum_scatter(
        partial_value.astype(jnp.bfloat16), "mlp", scatter_dimension=1, tiled=True
    ).astype(jnp.float32)
    scale_here = lax.dynamic_slice_in_dim(layer_scale, mlp_index * feat_width, feat_width)
    own_inputs = lax.dynamic_slice_in_dim(inputs, mlp_index * feat_width, feat_width, axis=1)
    patch_out = (own_inputs + scale_here * ffn_feats).astype(jnp.bfloat16)
    merged = patch_out.reshape(rows_here // 4, 4 * feat_width)
    weight_cols = projection.reshape(4 * feat_width, projection.shape[2])
    piece_rows = text_rows.shape[0]
    slot_count = destination.shape[0]
    bucket_count = req_count * mlp_count
    capacity = slot_count // bucket_count
    is_valid = destination >= 0
    piece_ids = jnp.where(is_valid, destination // piece_rows, -1)
    offsets = destination % piece_rows
    bucket_hit = piece_ids[:, None] == jnp.arange(bucket_count, dtype=jnp.int32)[None, :]
    first_off = jnp.min(jnp.where(bucket_hit, offsets[:, None], piece_rows), axis=0)
    counts = jnp.sum(bucket_hit.astype(jnp.int32), axis=0)
    slot_first = jnp.sum(jnp.where(bucket_hit, first_off[None, :], 0), axis=1)
    slot_rank = offsets - slot_first
    stream_ids = piece_ids // mlp_count
    piece_in = piece_ids % mlp_count
    rows_at = piece_in * (req_count * capacity) + stream_ids * capacity + slot_rank
    rows_at = jnp.where(is_valid, rows_at, bucket_count * capacity)
    sources = (
        jnp.full((bucket_count * capacity,), -1, jnp.int32)
        .at[rows_at]
        .set(jnp.arange(slot_count, dtype=jnp.int32), mode="drop")
    )
    every_row = lax.all_gather(merged, "req", axis=0, tiled=True)
    picked_rows = jnp.take(every_row, jnp.maximum(sources, 0), axis=0)
    picked_rows = jnp.where(sources[:, None] >= 0, picked_rows, jnp.zeros_like(picked_rows))
    summed = lax.psum_scatter(
        jnp.dot(picked_rows, weight_cols, preferred_element_type=jnp.float32).astype(jnp.bfloat16),
        "mlp",
        scatter_dimension=0,
        tiled=True,
    )
    arrived = lax.all_to_all(summed, "req", split_axis=0, concat_axis=1, tiled=True)
    bucket_here = req_index * mlp_count + mlp_index
    start_here = first_off[bucket_here]
    count_here = counts[bucket_here]
    positions = jnp.arange(piece_rows, dtype=jnp.int32) - start_here
    inside = (positions >= 0) & (positions < count_here)
    image_rows = jnp.take(arrived, jnp.clip(positions, 0, capacity - 1), axis=0)
    streams = jnp.where(inside[:, None], image_rows, text_rows)
    return (patch_out, streams)


def solution(mesh):
    return jax.shard_map(
        shards,
        mesh=mesh,
        in_specs=(
            P("req", None),
            P(),
            P(),
            P(None, ("req", "mlp")),
            P(None, ("req", "mlp")),
            P(None, ("req", "mlp")),
            P(),
            P(None, "mlp", "req"),
            P(("req", "mlp"), None),
            P(),
        ),
        out_specs=(P("req", "mlp"), P(("req", "mlp"), None)),
        check_vma=False,
    )
```

profile of v0, /device:TPU:0, one launch (start us, length us, event | category | flops | bytes accessed | tf_op | source)
XLA Modules:
  0.0 527.9 jit_solution(9855831558795438825)
XLA Ops:
  7.2 0.7 all-gather.5.cloned.1.call-update
  8.0 0.7 all-gather.7.cloned.1.call-update
  8.7 0.7 all-gather.9.cloned.1.call-update
  9.5 4.5 convert_reduce_fusion
  14.0 1.0 copy-done.1
  14.9 2.2 multiply_reduce_fusion
  17.1 66.4 %all-gather.5.cloned.1.call-done = bf16[4096,1024]{0,1:T(8,128)(2,1)} async-done(((bf16[4096,64]{0,1:T(8,128)(2,1)}), bf16[4096,1024]{0,1:T(8,128)(2,1)}) %all-gather.5.cloned.1.call-update) | async-done | bytes 8388624 | tf_op jit(solution)/shard_map/all_gather | solution.py:36
  83.5 14.4 %fusion.31 = f32[960,1024]{1,0:T(8,128)} fusion(bf16[4096,1024]{0,1:T(8,128)(2,1)} %all-gather.5.cloned.1.call-done, bf16[960,4096]{1,0:T(8,128)(2,1)} %param.10, f32[4096]{0:T(1024)S(1)} %copy-done.4, f32[4096]{0:T(1024)S(1)} %copy-done.5, f32[960]{0:T(1024)S(1)} %add_rsqrt_fusion, f32[960]{0:T(1024)S(1)} %broadcast_multiply_fusion), kind=kOutput, calls=%fused_computation.68 | convolution fusion | flops 8076656640 | bytes 20225536 | tf_op jit(solution)/shard_map/dot_general | solution.py:34
  97.9 58.2 %all-gather.7.cloned.1.call-done = bf16[4096,1024]{0,1:T(8,128)(2,1)} async-done(((bf16[4096,64]{0,1:T(8,128)(2,1)}), bf16[4096,1024]{0,1:T(8,128)(2,1)}) %all-gather.7.cloned.1.call-update) | async-done | bytes 8388624 | tf_op jit(solution)/shard_map/all_gather | solution.py:41
  156.1 72.6 %all-gather.9.cloned.1.call-done = bf16[4096,1024]{0,1:T(8,128)(2,1)} async-done(((bf16[4096,64]{0,1:T(8,128)(2,1)}), bf16[4096,1024]{0,1:T(8,128)(2,1)}) %all-gather.9.cloned.1.call-update) | async-done | bytes 8388624 | tf_op jit(solution)/shard_map/all_gather | solution.py:47
  228.7 25.9 %convolution_convert_fusion = bf16[960,4096]{1,0:T(8,128)(2,1)} fusion(bf16[4096,1024]{0,1:T(8,128)(2,1)} %all-gather.9.cloned.1.call-done, f32[960,1024]{1,0:T(8,128)} %fusion.31, bf16[4096,1024]{0,1:T(8,128)(2,1)} %all-gather.7.cloned.1.call-done, bf16[960,4096]{1,0:T(8,128)(2,1)} %param.10, f32[4096]{0:T(1024)S(1)} %copy-done.4, f32[4096]{0:T(1024)S(1)} %copy-done.5, ...), kind=kOutput, calls=%fused_computation.13 | convolution fusion | flops 16139550720 | bytes 36478464 | tf_op jit(solution)/shard_map/dot_general | solution.py:45
  254.7 11.3 %convert_element_type.26 = f32[960,4096]{1,0:T(8,128)} convert(bf16[960,4096]{1,0:T(8,128)(2,1)} %param.10) | non-fusion elementwise | flops 3932160 | bytes 23592960 | tf_op jit(solution)/shard_map/convert_element_type | solution.py:32
  266.0 0.8 dynamic_slice.13
  266.7 37.6 %reduce-scatter.3.cloned.1.call-done = bf16[960,512]{1,0:T(8,128)(2,1)} async-done(((bf16[960,4096]{1,0:T(8,128)(2,1)}), bf16[960,512]{1,0:T(8,128)(2,1)}) %reduce-scatter.3.cloned.1.call-update) | async-done | bytes 983056 | tf_op jit(solution)/shard_map/reduce_scatter | solution.py:52
  304.3 2.2 add_convert_fusion.1
  306.5 1.5 reshape.67
  308.1 2.5 select_reduce_fusion.1
  310.6 2.4 convert_reduce_fusion.1
  313.1 14.6 %scatter_custom_fusion = s32[3840]{0:T(1024)S(1)} fusion(s32[3840]{0:T(1024)S(1)} %compare_select_fusion, s32[3840]{0:T(1024)S(1)} %iota.16, s32[]{:T(128)} %constant.104.clone.1), kind=kCustom, calls=%fused_computation.51 | custom fusion | bytes 15364 | tf_op jit(solution)/shard_map/scatter | solution.py:79
  327.7 86.2 %all-gather.11.cloned.1.call-done = bf16[3840,2048]{1,0:T(8,128)(2,1)} async-done(((bf16[240,2048]{1,0:T(8,128)(2,1)}), bf16[3840,2048]{1,0:T(8,128)(2,1)}) %all-gather.11.cloned.1.call-update) | async-done | bytes 15728656 | tf_op jit(solution)/shard_map/all_gather | solution.py:81
  413.9 37.0 %gather_fusion = bf16[3840,2048]{1,0:T(8,128)(2,1)} fusion(bf16[3840,2048]{1,0:T(8,128)(2,1)} %all-gather.11.cloned.1.call-done, s32[4096]{0:T(1024)S(1)} %pad_clamp_fusion), kind=kCustom, calls=%fused_computation | custom fusion | bytes 31472640 | tf_op jit(solution)/shard_map/jit(_take)/gather | solution.py:82
  450.9 9.9 %fusion.7 = bf16[3840,256]{1,0:T(8,128)(2,1)} fusion(bf16[2048,256]{1,0:T(8,128)(2,1)S(1)} %bitcast.13, bf16[3840,2048]{1,0:T(8,128)(2,1)} %gather_fusion, pred[3840]{0:T(1024)(128)(4,1)S(1)} %get-tuple-element.5, pred[3840]{0:T(1024)(128)(4,1)S(1)} %get-tuple-element.4), kind=kOutput, calls=%fused_computation.14 | convolution fusion | flops 4043243520 | bytes 18750976 | tf_op jit(solution)/shard_map/dot_general | solution.py:85
  460.8 0.6 dynamic_slice.14
  461.4 0.6 dynamic_slice.15
  462.1 31.9 %reduce-scatter.5.cloned.1.call-done = bf16[480,256]{1,0:T(8,128)(2,1)} async-done(((bf16[3840,256]{1,0:T(8,128)(2,1)}), bf16[480,256]{1,0:T(8,128)(2,1)}) %reduce-scatter.5.cloned.1.call-update) | async-done | bytes 245776 | tf_op jit(solution)/shard_map/reduce_scatter | solution.py:84
  494.0 1.7 all_to_all.14
  495.7 6.9 %all-to-all-start = ((bf16[16,30,256]{2,1,0:T(8,128)(2,1)}), bf16[16,30,256]{2,1,0:T(8,128)(2,1)S(1)}, u32[]{:S(2)}, u32[]{:S(2)}) async-start(bf16[16,30,256]{2,1,0:T(8,128)(2,1)} %all_to_all.14), calls=%async_computation.2 | async-start | bytes 524288 | tf_op jit(solution)/shard_map/all_to_all | solution.py:90
  502.6 1.3 fusion.27
  503.9 0.6 compare_select_fusion.1
  504.6 6.5 %all-to-all-done = bf16[16,30,256]{2,1,0:T(8,128)(2,1)S(1)} async-done(((bf16[16,30,256]{2,1,0:T(8,128)(2,1)}), bf16[16,30,256]{2,1,0:T(8,128)(2,1)S(1)}, u32[]{:S(2)}, u32[]{:S(2)}) %all-to-all-start) | async-done | bytes 245792 | tf_op jit(solution)/shard_map/all_to_all | solution.py:90
  511.4 4.4 gather_fusion.1
  515.7 5.3 select_select_fusion
  (32 shorter events, 0.7 us)
Async XLA Ops:
  7.2 443.7 %copy-start = (bf16[4,512,256]{2,1,0:T(8,128)(2,1)S(1)}, bf16[4,512,256]{2,1,0:T(8,128)(2,1)}, u32[]{:S(2)}) copy-start(bf16[4,512,256]{2,1,0:T(8,128)(2,1)} %param.17) | copy-start | bytes 3145732
  7.2 76.3 %all-gather.5.cloned.1.call-start = ((), (), s32[]{:S(2)}) async-start(), calls=%async_computation.3 | async-start | bytes 8912896 | tf_op jit(solution)/shard_map/all_gather | solution.py:36
  7.9 148.2 %all-gather.7.cloned.1.call-start = ((), (), s32[]{:S(2)}) async-start(), calls=%async_computation.4 | async-start | bytes 8912896 | tf_op jit(solution)/shard_map/all_gather | solution.py:41
  8.7 220.1 %all-gather.9.cloned.1.call-start = ((), (), s32[]{:S(2)}) async-start(), calls=%async_computation.5 | async-start | bytes 8912896 | tf_op jit(solution)/shard_map/all_gather | solution.py:47
  9.4 294.9 %reduce-scatter.3.cloned.1.call-start = ((), (), s32[]{:S(2)}) async-start(), calls=%async_computation.6 | async-start | bytes 8847360 | tf_op jit(solution)/shard_map/reduce_scatter | solution.py:52
  9.4 5.5 %copy-start.1 = (bf16[960,4096]{1,0:T(8,128)(2,1)S(1)}, bf16[960,4096]{1,0:T(8,128)(2,1)}, u32[]{:S(2)}) copy-start(bf16[960,4096]{1,0:T(8,128)(2,1)} %param.10) | copy-start | bytes 23592964
  9.5 74.1 %copy-start.4 = (f32[4096]{0:T(1024)S(1)}, f32[4096]{0:T(1024)}, u32[]{:S(2)}) copy-start(f32[4096]{0:T(1024)} %param.12) | copy-start | bytes 49156
  9.5 74.1 %copy-start.5 = (f32[4096]{0:T(1024)S(1)}, f32[4096]{0:T(1024)}, u32[]{:S(2)}) copy-start(f32[4096]{0:T(1024)} %param.11) | copy-start | bytes 49156
  254.6 159.3 %all-gather.11.cloned.1.call-start = ((), (), s32[]{:S(2)}) async-start(), calls=%async_computation.7 | async-start | bytes 16711680 | tf_op jit(solution)/shard_map/all_gather | solution.py:81
  254.7 53.4 %copy-start.3 = (s32[3840]{0:T(1024)S(1)}, s32[3840]{0:T(1024)}, u32[]{:S(2)}) copy-start(s32[3840]{0:T(1024)} %param.19) | copy-start | bytes 46084
  306.5 144.4 %copy-start.2 = (bf16[960,512]{1,0:T(8,128)(2,1)}, bf16[960,512]{1,0:T(8,128)(2,1)S(1)}, u32[]{:S(2)}) copy-start(bf16[960,512]{1,0:T(8,128)(2,1)S(1)} %add_convert_fusion.1) | copy-start | bytes 2949124
  308.0 186.0 %reduce-scatter.5.cloned.1.call-start = ((), (), s32[]{:S(2)}) async-start(), calls=%async_computation.8 | async-start | bytes 2211840 | tf_op jit(solution)/shard_map/reduce_scatter | solution.py:84
  495.7 15.4 %all-to-all-start = ((bf16[16,30,256]{2,1,0:T(8,128)(2,1)}), bf16[16,30,256]{2,1,0:T(8,128)(2,1)S(1)}, u32[]{:S(2)}, u32[]{:S(2)}) async-start(bf16[16,30,256]{2,1,0:T(8,128)(2,1)} %all_to_all.14), calls=%async_computation.2 | async-start | bytes 524288 | tf_op jit(solution)/shard_map/all_to_all | solution.py:90
Sparse Core Ops, SparseCore 0:
  10.2 73.3 all-gather.4
  85.7 70.4 all-gather.6
  158.3 70.4 all-gather.8
  254.7 49.5 reduce-scatter.2
  308.2 105.6 all-gather.10
  460.9 33.0 reduce-scatter.4
where the time goes:
time: 528 us
  waiting for transfers between devices  362 us (69%)
  local copies, waits for them, and re-layouts  62.5 us (12%)
  matrix products  50.1 us (9%)
  other arithmetic  32.3 us (6%)
  between operations  14.3 us (3%)
  starting transfers between devices  7.14 us (1%)
    all_gather x1, waiting for transfers between devices, shards(): every_row = lax.all_gather(merged, 'req', axis=0, tiled=True)  86.2 us
    all_gather x1, waiting for transfers between devices, shards(): lax.all_gather(down_weight, 'req', axis=1, tiled=True)  72.6 us
    all_gather x1, waiting for transfers between devices, shards(): lax.all_gather(gate_weight, 'req', axis=1, tiled=True)  66.4 us
    all_gather x1, waiting for transfers between devices, shards(): lax.all_gather(up_weight, 'req', axis=1, tiled=True)  58.2 us
    reduce_scatter x1, waiting for transfers between devices, shards(): lax.psum_scatter(partial_value.astype(jnp.bfloat16), 'mlp', scatter_dimen...  37.6 us
    gather x1, local copies, waits for them, and re-layouts, shards(): picked_rows = jnp.take(every_row, jnp.maximum(sources, 0), axis=0)  37 us
    reduce_scatter x1, waiting for transfers between devices, shards(): lax.psum_scatter(jnp.dot(picked_rows, weight_cols, preferred_element_type...  31.9 us
    dot_general x1, matrix products, shards(): lax.dot_general(hidden, lax.all_gather(down_weight, 'req', axis=1, tiled=...  25.9 us
  transfers between devices with their start and end apart: 7, of which 7 were waited for; matrix products, arithmetic and copies ran while one was open for 11% of the time, Pallas kernels for 0%

commit v1 on v0

--- a/solution.py
+++ b/solution.py
@@ -2,6 +2,12 @@
 import jax.numpy as jnp
 from jax import lax
 from jax.sharding import PartitionSpec as P
+
+
+def tiled_gather(x, axis, dim):
+    peers = lax.axis_size(axis)
+    repeats = [peers if d == dim else 1 for d in range(x.ndim)]
+    return lax.all_to_all(jnp.tile(x, repeats), axis, split_axis=dim, concat_axis=dim, tiled=True)
 
 
 def layer_norm(values, norm_gain, norm_bias):
@@ -44,7 +50,7 @@
     hidden = (jax.nn.silu(gate_act) * up_act).astype(jnp.bfloat16)
     ffn_local = lax.dot_general(
         hidden,
-        lax.all_gather(down_weight, "req", axis=1, tiled=True),
+        tiled_gather(down_weight, "req", 1),
         (((1,), (1,)), ((), ())),
         preferred_element_type=jnp.float32,
     )

time: 528 us -> 570 us (1.080)
  waiting for transfers between devices: 362 us -> 387 us
  starting transfers between devices: 7.14 us -> 15.2 us
    all_gather x1, waiting for transfers between devices: 66.4 us -> 163 us  [shards(): lax.all_gather(gate_weight, 'req', axis=1, tiled=True)]
    all_gather x1 -> x0, waiting for transfers between devices: 72.6 us -> none  [shards(): lax.all_gather(down_weight, 'req', axis=1, tiled=True)]
    all_to_all x0 -> x1, starting transfers between devices: none -> 8.01 us  [tiled_gather(): lax.all_to_all(jnp.tile(x, repeats), axis, split_axis=dim, concat_axis=di...]
  transfers between devices with their start and end apart: 7 -> 7, of which waited for: 7 -> 6; matrix products, arithmetic and copies ran while one was open for 11% -> 11% of each run, Pallas kernels for 0% -> 0%
where the time goes in v1:
time: 570 us; the launch traced here: 569 us
  waiting for transfers between devices  387 us (68%)
  local copies, waits for them, and re-layouts  66.7 us (12%)
  matrix products  50.2 us (9%)
  other arithmetic  35.6 us (6%)
  starting transfers between devices  15.2 us (3%)
  between operations  14 us (2%)
    all_gather x1, waiting for transfers between devices, shards(): lax.all_gather(gate_weight, 'req', axis=1, tiled=True)  163 us
    all_gather x1, waiting for transfers between devices, shards(): every_row = lax.all_gather(merged, 'req', axis=0, tiled=True)  86.2 us
    all_gather x1, waiting for transfers between devices, shards(): lax.all_gather(up_weight, 'req', axis=1, tiled=True)  60.4 us
    reduce_scatter x1, waiting for transfers between devices, shards(): lax.psum_scatter(partial_value.astype(jnp.bfloat16), 'mlp', scatter_dimen...  37.6 us
    gather x1, local copies, waits for them, and re-layouts, shards(): picked_rows = jnp.take(every_row, jnp.maximum(sources, 0), axis=0)  37 us
    reduce_scatter x1, waiting for transfers between devices, shards(): lax.psum_scatter(jnp.dot(picked_rows, weight_cols, preferred_element_type...  31.9 us
    dot_general x1, matrix products, shards(): lax.dot_general(hidden, tiled_gather(down_weight, 'req', 1), (((1,), (1,)...  25.9 us
    scatter x1, local copies, waits for them, and re-layouts, shards(): sources = jnp.full((bucket_count * capacity,), -1, jnp.int32).at[rows_at]...  14.6 us
  transfers between devices with their start and end apart: 7, of which 6 were waited for; matrix products, arithmetic and copies ran while one was open for 11% of the time, Pallas kernels for 0%

profile of v1, /device:TPU:0, one launch (start us, length us, event | category | flops | bytes accessed | tf_op | source)
XLA Modules:
  0.0 568.9 jit_solution(5689665917375988206)
XLA Ops:
  7.2 0.7 all-gather.4.cloned.1.call-update
  8.0 0.7 all-gather.6.cloned.1.call-update
  8.7 5.3 tile.2
  14.0 8.0 %all-to-all-start = ((bf16[4096,16,64]{0,2,1:T(8,128)(2,1)}), bf16[4096,16,64]{0,2,1:T(8,128)(2,1)}, u32[]{:S(2)}, u32[]{:S(2)}) async-start(bf16[4096,16,64]{0,2,1:T(8,128)(2,1)} %tile.2), calls=%async_computation | async-start | bytes 16777216 | tf_op jit(solution)/shard_map/all_to_all | solution.py:10
  22.1 4.6 convert_reduce_fusion
  26.7 5.4 multiply_reduce_fusion
  32.2 163.1 %all-gather.4.cloned.1.call-done = bf16[4096,1024]{0,1:T(8,128)(2,1)} async-done(((bf16[4096,64]{0,1:T(8,128)(2,1)}), bf16[4096,1024]{0,1:T(8,128)(2,1)}) %all-gather.4.cloned.1.call-update) | async-done | bytes 8388624 | tf_op jit(solution)/shard_map/all_gather | solution.py:42
  195.3 14.4 %fusion.31 = f32[960,1024]{1,0:T(8,128)} fusion(bf16[4096,1024]{0,1:T(8,128)(2,1)} %all-gather.4.cloned.1.call-done, bf16[960,4096]{1,0:T(8,128)(2,1)} %param.10, f32[4096]{0:T(1024)S(1)} %copy-done.3, f32[4096]{0:T(1024)S(1)} %copy-done.4, f32[960]{0:T(1024)S(1)} %add_rsqrt_fusion, f32[960]{0:T(1024)S(1)} %broadcast_multiply_fusion), kind=kOutput, calls=%fused_computation.68 | convolution fusion | flops 8076656640 | bytes 20225536 | tf_op jit(solution)/shard_map/dot_general | solution.py:40
  209.7 60.4 %all-gather.6.cloned.1.call-done = bf16[4096,1024]{0,1:T(8,128)(2,1)} async-done(((bf16[4096,64]{0,1:T(8,128)(2,1)}), bf16[4096,1024]{0,1:T(8,128)(2,1)}) %all-gather.6.cloned.1.call-update) | async-done | bytes 8388624 | tf_op jit(solution)/shard_map/all_gather | solution.py:47
  270.1 25.9 %convolution_convert_fusion = bf16[960,4096]{1,0:T(8,128)(2,1)} fusion(bf16[4096,1024]{0,1:T(8,128)(2,1)} %bitcast, f32[960,1024]{1,0:T(8,128)} %fusion.31, bf16[4096,1024]{0,1:T(8,128)(2,1)} %all-gather.6.cloned.1.call-done, bf16[960,4096]{1,0:T(8,128)(2,1)} %param.10, f32[4096]{0:T(1024)S(1)} %copy-done.3, f32[4096]{0:T(1024)S(1)} %copy-done.4, ...), kind=kOutput, calls=%fused_computation.13 | convolution fusion | flops 16139550720 | bytes 36478464 | tf_op jit(solution)/shard_map/dot_general | solution.py:51
  296.0 11.3 %convert_element_type.26 = f32[960,4096]{1,0:T(8,128)} convert(bf16[960,4096]{1,0:T(8,128)(2,1)} %param.10) | non-fusion elementwise | flops 3932160 | bytes 23592960 | tf_op jit(solution)/shard_map/convert_element_type | solution.py:38
  307.3 0.8 dynamic_slice.13
  308.1 37.6 %reduce-scatter.3.cloned.1.call-done = bf16[960,512]{1,0:T(8,128)(2,1)} async-done(((bf16[960,4096]{1,0:T(8,128)(2,1)}), bf16[960,512]{1,0:T(8,128)(2,1)}) %reduce-scatter.3.cloned.1.call-update) | async-done | bytes 983056 | tf_op jit(solution)/shard_map/reduce_scatter | solution.py:58
  345.7 2.2 add_convert_fusion.1
  347.8 1.5 reshape.74
  349.5 2.5 select_reduce_fusion.1
  352.0 2.4 convert_reduce_fusion.1
  354.4 14.6 %scatter_custom_fusion = s32[3840]{0:T(1024)S(1)} fusion(s32[3840]{0:T(1024)S(1)} %compare_select_fusion, s32[3840]{0:T(1024)S(1)} %iota.16, s32[]{:T(128)} %constant.104.clone.1), kind=kCustom, calls=%fused_computation.51 | custom fusion | bytes 15364 | tf_op jit(solution)/shard_map/scatter | solution.py:85
  369.1 86.2 %all-gather.8.cloned.1.call-done = bf16[3840,2048]{1,0:T(8,128)(2,1)} async-done(((bf16[240,2048]{1,0:T(8,128)(2,1)}), bf16[3840,2048]{1,0:T(8,128)(2,1)}) %all-gather.8.cloned.1.call-update) | async-done | bytes 15728656 | tf_op jit(solution)/shard_map/all_gather | solution.py:87
  455.3 37.0 %gather_fusion = bf16[3840,2048]{1,0:T(8,128)(2,1)} fusion(bf16[3840,2048]{1,0:T(8,128)(2,1)} %all-gather.8.cloned.1.call-done, s32[4096]{0:T(1024)S(1)} %pad_clamp_fusion), kind=kCustom, calls=%fused_computation | custom fusion | bytes 31472640 | tf_op jit(solution)/shard_map/jit(_take)/gather | solution.py:88
  492.2 9.9 %fusion.7 = bf16[3840,256]{1,0:T(8,128)(2,1)} fusion(bf16[2048,256]{1,0:T(8,128)(2,1)S(1)} %bitcast.14, bf16[3840,2048]{1,0:T(8,128)(2,1)} %gather_fusion, pred[3840]{0:T(1024)(128)(4,1)S(1)} %get-tuple-element.5, pred[3840]{0:T(1024)(128)(4,1)S(1)} %get-tuple-element.4), kind=kOutput, calls=%fused_computation.14 | convolution fusion | flops 4043243520 | bytes 18750976 | tf_op jit(solution)/shard_map/dot_general | solution.py:91
  502.2 0.6 dynamic_slice.14
  502.8 0.6 dynamic_slice.15
  503.4 31.9 %reduce-scatter.5.cloned.1.call-done = bf16[480,256]{1,0:T(8,128)(2,1)} async-done(((bf16[3840,256]{1,0:T(8,128)(2,1)}), bf16[480,256]{1,0:T(8,128)(2,1)}) %reduce-scatter.5.cloned.1.call-update) | async-done | bytes 245776 | tf_op jit(solution)/shard_map/reduce_scatter | solution.py:90
  535.3 1.7 all_to_all.22
  537.0 7.0 %all-to-all-start.1 = ((bf16[16,30,256]{2,1,0:T(8,128)(2,1)}), bf16[16,30,256]{2,1,0:T(8,128)(2,1)S(1)}, u32[]{:S(2)}, u32[]{:S(2)}) async-start(bf16[16,30,256]{2,1,0:T(8,128)(2,1)} %all_to_all.22), calls=%async_computation.3 | async-start | bytes 524288 | tf_op jit(solution)/shard_map/all_to_all | solution.py:96
  544.0 1.2 fusion.27
  545.2 0.6 compare_select_fusion.1
  545.8 6.7 %all-to-all-done.1 = bf16[16,30,256]{2,1,0:T(8,128)(2,1)S(1)} async-done(((bf16[16,30,256]{2,1,0:T(8,128)(2,1)}), bf16[16,30,256]{2,1,0:T(8,128)(2,1)S(1)}, u32[]{:S(2)}, u32[]{:S(2)}) %all-to-all-start.1) | async-done | bytes 245792 | tf_op jit(solution)/shard_map/all_to_all | solution.py:96
  552.4 0.1 copy.15
  552.7 4.4 gather_fusion.1
  557.1 5.3 select_select_fusion
  (30 shorter events, 0.5 us)
Async XLA Ops:
  7.2 485.1 %copy-start = (bf16[4,512,256]{2,1,0:T(8,128)(2,1)S(1)}, bf16[4,512,256]{2,1,0:T(8,128)(2,1)}, u32[]{:S(2)}) copy-start(bf16[4,512,256]{2,1,0:T(8,128)(2,1)} %param.17) | copy-start | bytes 3145732
  7.2 188.1 %all-gather.4.cloned.1.call-start = ((), (), s32[]{:S(2)}) async-start(), calls=%async_computation.4 | async-start | bytes 8912896 | tf_op jit(solution)/shard_map/all_gather | solution.py:42
  7.9 262.2 %all-gather.6.cloned.1.call-start = ((), (), s32[]{:S(2)}) async-start(), calls=%async_computation.5 | async-start | bytes 8912896 | tf_op jit(solution)/shard_map/all_gather | solution.py:47
  14.0 195.7 %all-to-all-start = ((bf16[4096,16,64]{0,2,1:T(8,128)(2,1)}), bf16[4096,16,64]{0,2,1:T(8,128)(2,1)}, u32[]{:S(2)}, u32[]{:S(2)}) async-start(bf16[4096,16,64]{0,2,1:T(8,128)(2,1)} %tile.2), calls=%async_computation | async-start | bytes 16777216 | tf_op jit(solution)/shard_map/all_to_all | solution.py:10
  22.0 173.3 %copy-start.3 = (f32[4096]{0:T(1024)S(1)}, f32[4096]{0:T(1024)}, u32[]{:S(2)}) copy-start(f32[4096]{0:T(1024)} %param.12) | copy-start | bytes 49156
  22.0 173.3 %copy-start.4 = (f32[4096]{0:T(1024)S(1)}, f32[4096]{0:T(1024)}, u32[]{:S(2)}) copy-start(f32[4096]{0:T(1024)} %param.11) | copy-start | bytes 49156
  22.0 323.6 %reduce-scatter.3.cloned.1.call-start = ((), (), s32[]{:S(2)}) async-start(), calls=%async_computation.6 | async-start | bytes 8847360 | tf_op jit(solution)/shard_map/reduce_scatter | solution.py:58
  296.0 159.3 %all-gather.8.cloned.1.call-start = ((), (), s32[]{:S(2)}) async-start(), calls=%async_computation.7 | async-start | bytes 16711680 | tf_op jit(solution)/shard_map/all_gather | solution.py:87
  296.0 53.4 %copy-start.2 = (s32[3840]{0:T(1024)S(1)}, s32[3840]{0:T(1024)}, u32[]{:S(2)}) copy-start(s32[3840]{0:T(1024)} %param.19) | copy-start | bytes 46084
  347.8 144.4 %copy-start.1 = (bf16[960,512]{1,0:T(8,128)(2,1)}, bf16[960,512]{1,0:T(8,128)(2,1)S(1)}, u32[]{:S(2)}) copy-start(bf16[960,512]{1,0:T(8,128)(2,1)S(1)} %add_convert_fusion.1) | copy-start | bytes 2949124
  349.4 185.9 %reduce-scatter.5.cloned.1.call-start = ((), (), s32[]{:S(2)}) async-start(), calls=%async_computation.8 | async-start | bytes 2211840 | tf_op jit(solution)/shard_map/reduce_scatter | solution.py:90
  537.0 15.4 %all-to-all-start.1 = ((bf16[16,30,256]{2,1,0:T(8,128)(2,1)}), bf16[16,30,256]{2,1,0:T(8,128)(2,1)S(1)}, u32[]{:S(2)}, u32[]{:S(2)}) async-start(bf16[16,30,256]{2,1,0:T(8,128)(2,1)} %all_to_all.22), calls=%async_computation.3 | async-start | bytes 524288 | tf_op jit(solution)/shard_map/all_to_all | solution.py:96
Sparse Core Ops, SparseCore 0:
  10.2 185.1 all-gather.3
  197.5 72.5 all-gather.5
  296.1 49.5 reduce-scatter.2
  349.5 105.6 all-gather.7
  502.3 32.9 reduce-scatter.4
